TPU v7x, 32 devices: a whole 2x2x4 slice. The times are simulated.
32 devices in a mesh: seq: 4 (over z), tp: 8 (over y, x, core).
Axes of the slice: x: 2, y: 2, z: 4, core: 2. Of those that a mesh axis runs over, the one named last changes fastest.
Arguments:
- tokens: bfloat16 [1024, 8192], P('tp', 'seq'), may hold values from -6 to 6
- gate_weight: bfloat16 [8192, 14336], P('seq', 'tp'), may hold values from -0.0625 to 0.0625
- up_weight: bfloat16 [8192, 14336], P('seq', 'tp'), may hold values from -0.0625 to 0.0625
- down_pool: bfloat16 [64, 64, 8192], P('tp', None, 'seq'), may hold values from -0.0625 to 0.0625
- up_pool: bfloat16 [64, 2, 64, 14336], P('seq', None, None, 'tp'), may hold values from -0.75 to 0.75
- req_len: int32 [4], replicated, may hold values from 1 to 4, 8 in all
- req_adapter: int32 [4], replicated, may hold values from 0 to 63
- owner_slot: int32 [64], replicated, may hold values from 0 to 63, each once
Outputs:
- hidden: bfloat16 [1024, 14336], P('seq', 'tp')
Inputs may be any that keep to these rules, and one draw needn't show every extreme that they name: `req_len`: lengths of the requests in segments, summing to 8; the longest is exactly 4. `req_adapter`: adapter ids; an adapter may serve several requests. `owner_slot`: each pool slot once.
All inputs are finite; a program needn't handle non-finite values.
Results may differ from a plain program's by a relative error of at most 0.015.
Values may be sent and summed in bfloat16 or wider, within the bound.
No kernel may reach another device: no remote copies, remote signals or barrier semaphores. Data moves between devices by JAX's collectives and lax.ppermute only.
A program may use at most 128 MiB of HBM per device.

v0:
```python
import jax
import jax.numpy as jnp
from jax import lax
from jax.sharding import PartitionSpec as P

SEG_ROWS = 128
low_rank_scale = 0.5


def segment_slots(req_len, req_adapter, owner_slot, segs):
    ends = jnp.cumsum(req_len)
    segment = jnp.arange(segs, dtype=jnp.int32)
    seg_request = jnp.sum((ends[None, :] <= segment[:, None]).astype(jnp.int32), axis=1)
    return jnp.take(owner_slot, jnp.take(req_adapter, seg_request))


def shards(tokens, gate_weight, up_weight, down_pool, up_pool, req_len, req_adapter, owner_slot):
    nseq = lax.axis_size("seq")
    ntp = lax.axis_size("tp")
    segs = tokens.shape[0] // SEG_ROWS * ntp
    seg_slot = segment_slots(req_len, req_adapter, owner_slot, segs)
    per_tp = down_pool.shape[0]
    per_seq = up_pool.shape[0]
    width = tokens.shape[1]
    half_width = gate_weight.shape[1]
    rank_size = down_pool.shape[1]
    own_segs = segs // nseq
    own_rows = own_segs * SEG_ROWS
    held_down = seg_slot // per_tp == lax.axis_index("tp")
    picked_down = jnp.take(down_pool, seg_slot % per_tp, axis=0).astype(jnp.float32)
    table_down = jnp.where(held_down[:, None, None], picked_down, 0.0)
    downs = lax.psum(table_down.astype(jnp.bfloat16), "tp")
    held_up = seg_slot // per_seq == lax.axis_index("seq")
    picked_up = jnp.take(up_pool, seg_slot % per_seq, axis=0).astype(jnp.float32)
    table_up = jnp.where(held_up[:, None, None, None], picked_up, 0.0)
    ups_own = lax.psum_scatter(
        table_up.astype(jnp.bfloat16), "seq", scatter_dimension=0, tiled=True
    )
    gathered = lax.all_gather(tokens, "tp", axis=0, tiled=True)
    inner_part = jnp.einsum(
        "kqd,krd->kqr",
        gathered.reshape(segs, SEG_ROWS, width),
        downs,
        preferred_element_type=jnp.float32,
    )
    inner_part = lax.optimization_barrier(inner_part.astype(jnp.bfloat16)).astype(jnp.float32)
    flat = inner_part.reshape(-1, 128)
    flat_own = own_rows * rank_size // 128
    inner_total = lax.psum(flat.astype(jnp.bfloat16), "seq").astype(jnp.float32)
    inner_own = lax.dynamic_slice_in_dim(inner_total, lax.axis_index("seq") * flat_own, flat_own, 0)
    inner_iteration = inner_own.astype(jnp.bfloat16).reshape(own_segs, SEG_ROWS, rank_size)
    low_rank_delta = jnp.einsum(
        "vcz,vwzd->vcwd", inner_iteration, ups_own, preferred_element_type=jnp.float32
    ).reshape(own_rows, 2, half_width)
    reduced_total = lax.psum_scatter(
        jnp.concatenate(
            [
                jnp.dot(gathered, gate_weight, preferred_element_type=jnp.float32),
                jnp.dot(gathered, up_weight, preferred_element_type=jnp.float32),
            ],
            axis=1,
        ).astype(jnp.bfloat16),
        "seq",
        scatter_dimension=0,
        tiled=True,
    ).astype(jnp.float32)
    gate_preactivation = reduced_total[:, :half_width] + low_rank_scale * low_rank_delta[:, 0]
    up_preactivation = reduced_total[:, half_width:] + low_rank_scale * low_rank_delta[:, 1]
    return (jax.nn.silu(gate_preactivation) * up_preactivation).astype(jnp.bfloat16)


def solution(mesh):
    placed = (
        P("tp", "seq"),
        P("seq", "tp"),
        P("seq", "tp"),
        P("tp", None, "seq"),
        P("seq", None, None, "tp"),
        P(),
        P(),
        P(),
    )
    return jax.shard_map(
        shards, mesh=mesh, in_specs=placed, out_specs=P("seq", "tp"), check_vma=False
    )
```

profile of v0, /device:TPU:0, one launch (start us, length us, event | category | flops | bytes accessed | tf_op | source)
XLA Modules:
  0.0 369.6 jit_solution(8576012177038805279)
XLA Ops:
  6.5 1.0 reduce-window.8
  7.6 1.3 gather_fusion
  8.9 1.3 gather_fusion.1
  10.3 2.0 gather_fusion.2
  12.4 3.6 select_convert_fusion.1
  16.1 0.7 all-gather.2.cloned.1.call-update
  16.9 5.8 %gather_fusion.3 = bf16[8,2,64,1792]{3,2,1,0:T(8,128)(2,1)} fusion(bf16[16,2,64,1792]{3,2,1,0:T(8,128)(2,1)} %param.12, s32[1024]{0:T(1024)S(1)} %pad_clamp_fusion), kind=kCustom, calls=%fused_computation.3 | custom fusion | bytes 7340064 | tf_op jit(solution)/shard_map/jit(_take)/gather | solution.py:34
  22.6 57.7 %all-reduce.3.cloned.1.call-done = bf16[8,64,2048]{2,1,0:T(8,128)(2,1)} async-done(((bf16[8,64,2048]{2,1,0:T(8,128)(2,1)}), bf16[8,64,2048]{2,1,0:T(8,128)(2,1)}) %all-reduce.3.cloned.1.call-update) | async-done | bytes 2097168 | tf_op jit(solution)/shard_map/psum | solution.py:32
  80.3 37.8 %all-gather.2.cloned.1.call-done = bf16[1024,2048]{1,0:T(8,128)(2,1)} async-done(((bf16[128,2048]{1,0:T(8,128)(2,1)}), bf16[1024,2048]{1,0:T(8,128)(2,1)}) %all-gather.2.cloned.1.call-update) | async-done | bytes 4194320 | tf_op jit(solution)/shard_map/all_gather | solution.py:39
  118.2 4.4 %fusion.6 = bf16[8,128,64]{1,2,0:T(8,128)(2,1)S(1)} fusion(bf16[8,64,2048]{2,1,0:T(8,128)(2,1)} %all-reduce.3.cloned.1.call-done, bf16[8,128,2048]{2,1,0:T(8,128)(2,1)} %bitcast.61), kind=kOutput, calls=%fused_computation.18 | convolution fusion | flops 268500992 | bytes 6422528 | tf_op jit(solution)/shard_map/kqd,krd->kqr/dot_general | solution.py:40
  122.5 0.2 copy.13
  122.7 0.8 convert_element_type.45
  123.6 4.9 %select_convert_fusion = bf16[8,2,64,1792]{3,2,1,0:T(8,128)(2,1)} fusion(bf16[8,2,64,1792]{3,2,1,0:T(8,128)(2,1)} %gather_fusion.3, pred[8]{0:T(512)(128)(4,1)S(1)} %get-tuple-element.10, pred[8]{0:T(512)(128)(4,1)S(1)} %get-tuple-element.11), kind=kLoop, calls=%fused_computation.5 | loop fusion | flops 7340032 | bytes 7340048 | tf_op jit(solution)/shard_map/convert_element_type | solution.py:37
  128.6 13.1 %convolution_convert_fusion = bf16[1024,1792]{1,0:T(8,128)(2,1)} fusion(bf16[1024,2048]{1,0:T(8,128)(2,1)} %all-gather.2.cloned.1.call-done, bf16[2048,1792]{1,0:T(8,128)(2,1)} %param.10), kind=kOutput, calls=%fused_computation.7 | convolution fusion | flops 7518027776 | bytes 15204352 | tf_op jit(solution)/shard_map/dot_general | solution.py:59
  141.7 12.3 %convolution_convert_fusion.1 = bf16[1024,1792]{1,0:T(8,128)(2,1)} fusion(bf16[1024,2048]{1,0:T(8,128)(2,1)S(1)} %copy-done.3, bf16[2048,1792]{1,0:T(8,128)(2,1)} %param.9), kind=kOutput, calls=%fused_computation.8 | convolution fusion | flops 7518027776 | bytes 15204352 | tf_op jit(solution)/shard_map/dot_general | solution.py:58
  154.0 6.6 %pad_maximum_fusion = bf16[1024,3584]{1,0:T(8,128)(2,1)} fusion(bf16[1024,1792]{1,0:T(8,128)(2,1)} %convolution_convert_fusion, bf16[1024,1792]{1,0:T(8,128)(2,1)} %convolution_convert_fusion.1), kind=kLoop, calls=%fused_computation.4 | loop fusion | flops 14680064 | bytes 14680064 | tf_op jit(solution)/shard_map/concatenate | solution.py:56
  160.6 0.8 convert_convert_fusion
  161.4 0.1 reshape.295
  161.5 67.0 %reduce-scatter.5.cloned.1.call-done = bf16[2,2,64,1792]{3,2,1,0:T(8,128)(2,1)} async-done(((bf16[8,2,64,1792]{3,2,1,0:T(8,128)(2,1)}), bf16[2,2,64,1792]{3,2,1,0:T(8,128)(2,1)}) %reduce-scatter.5.cloned.1.call-update) | async-done | bytes 917520 | tf_op jit(solution)/shard_map/reduce_scatter | solution.py:36
  228.5 3.7 %fusion.7 = f32[2,128,2,1792]{3,1,0,2:T(8,128)} fusion(bf16[2,2,64,1792]{3,2,1,0:T(8,128)(2,1)} %reduce-scatter.5.cloned.1.call-done, bf16[2,128,64]{2,1,0:T(8,128)(2,1)S(1)} %reshape.295), kind=kOutput, calls=%fused_computation.19 | convolution fusion | flops 117440512 | bytes 4620288 | tf_op jit(solution)/shard_map/vcz,vwzd->vcwd/dot_general | solution.py:52
  232.2 126.7 %reduce-scatter.3.cloned.1.call-done = bf16[256,3584]{1,0:T(8,128)(2,1)} async-done(((bf16[1024,3584]{1,0:T(8,128)(2,1)}), bf16[256,3584]{1,0:T(8,128)(2,1)}) %reduce-scatter.3.cloned.1.call-update) | async-done | bytes 1835024 | tf_op jit(solution)/shard_map/reduce_scatter | solution.py:55
  358.9 2.1 convert_element_type.39
  361.0 0.5 copy-done.2
  361.5 1.6 fusion.3
  (28 shorter events, 0.5 us)
Async XLA Ops:
  6.5 3.8 %copy-start = (bf16[8,64,2048]{2,1,0:T(8,128)(2,1)S(1)}, bf16[8,64,2048]{2,1,0:T(8,128)(2,1)}, u32[]{:S(2)}) copy-start(bf16[8,64,2048]{2,1,0:T(8,128)(2,1)} %param.11) | copy-start | bytes 6291460
  6.5 73.8 %all-reduce.3.cloned.1.call-start = ((), (), s32[]{:S(2)}) async-start(), calls=%async_computation.4 | async-start | bytes 4194304 | tf_op jit(solution)/shard_map/psum | solution.py:32
  16.0 102.1 %all-gather.2.cloned.1.call-start = ((), (), s32[]{:S(2)}) async-start(), calls=%async_computation.2 | async-start | bytes 4718592 | tf_op jit(solution)/shard_map/all_gather | solution.py:39
  16.8 143.9 %all-reduce.5.cloned.1.call-start = ((), (), s32[]{:S(2)}) async-start(), calls=%async_computation.5 | async-start | bytes 262144 | tf_op jit(solution)/shard_map/psum | solution.py:49
  123.6 104.9 %reduce-scatter.5.cloned.1.call-start = ((), (), s32[]{:S(2)}) async-start(), calls=%async_computation.6 | async-start | bytes 4587520 | tf_op jit(solution)/shard_map/reduce_scatter | solution.py:36
  128.6 230.3 %reduce-scatter.3.cloned.1.call-start = ((), (), s32[]{:S(2)}) async-start(), calls=%async_computation.3 | async-start | bytes 9175040 | tf_op jit(solution)/shard_map/reduce_scatter | solution.py:55
  128.6 13.1 %copy-start.3 = (bf16[1024,2048]{1,0:T(8,128)(2,1)S(1)}, bf16[1024,2048]{1,0:T(8,128)(2,1)}, u32[]{:S(2)}) copy-start(bf16[1024,2048]{1,0:T(8,128)(2,1)} %all-gather.2.cloned.1.call-done) | copy-start | bytes 12582916
  358.9 2.6 copy-start.2
  361.0 2.1 copy-start.1
Sparse Core Ops, SparseCore 0:
  16.2 64.1 all-reduce.2
  82.2 35.9 all-gather.1
  123.7 34.4 all-reduce.4
  160.4 68.0 reduce-scatter.4
  230.7 128.1 reduce-scatter.2
where the time goes:
time: 370 us
  waiting for transfers between devices  290 us (78%)
  matrix products  33.4 us (9%)
  other arithmetic  20.8 us (6%)
  between operations  13.3 us (4%)
  local copies, waits for them, and re-layouts  12 us (3%)
    reduce_scatter x1, waiting for transfers between devices, shards(): lax.psum_scatter(jnp.concatenate([jnp.dot(gathered, gate_weight, preferre...  127 us
    reduce_scatter x1, waiting for transfers between devices, shards(): lax.psum_scatter(table_up.astype(jnp.bfloat16), 'seq', scatter_dimension=...  67 us
    psum x1, waiting for transfers between devices, shards(): downs = lax.psum(table_down.astype(jnp.bfloat16), 'tp')  57.7 us
    all_gather x1, waiting for transfers between devices, shards(): gathered = lax.all_gather(tokens, 'tp', axis=0, tiled=True)  37.8 us
    dot_general x1, matrix products, shards(): jnp.dot(gathered, up_weight, preferred_element_type=jnp.float32)  13.1 us
    dot_general x1, matrix products, shards(): jnp.dot(gathered, gate_weight, preferred_element_type=jnp.float32)  12.3 us
  transfers between devices with their start and end apart: 5, of which 4 were waited for; matrix products, arithmetic and copies ran while one was open for 13% of the time, Pallas kernels for 0%

commit v1 on v0

--- a/solution.py
+++ b/solution.py
@@ -29,7 +29,9 @@
     held_down = seg_slot // per_tp == lax.axis_index("tp")
     picked_down = jnp.take(down_pool, seg_slot % per_tp, axis=0).astype(jnp.float32)
     table_down = jnp.where(held_down[:, None, None], picked_down, 0.0)
-    downs = lax.psum(table_down.astype(jnp.bfloat16), "tp")
+    block = table_down.astype(jnp.bfloat16)
+    terms = lax.all_gather(block, "tp")
+    downs = jnp.sum(terms, axis=0)
     held_up = seg_slot // per_seq == lax.axis_index("seq")
     picked_up = jnp.take(up_pool, seg_slot % per_seq, axis=0).astype(jnp.float32)
     table_up = jnp.where(held_up[:, None, None, None], picked_up, 0.0)

time: 370 us -> 389 us (1.051)
  other arithmetic: 20.8 us -> 32.2 us
  waiting for transfers between devices: 290 us -> 300 us
    psum x1 -> x0, waiting for transfers between devices: 57.7 us -> none  [shards(): downs = lax.psum(table_down.astype(jnp.bfloat16), 'tp')]
    all_gather x0 -> x1, waiting for transfers between devices: none -> 53.9 us  [shards(): terms = lax.all_gather(block, 'tp')]
    psum x1, waiting for transfers between devices: 0.02 us -> 33.5 us  [shards(): inner_total = lax.psum(flat.astype(jnp.bfloat16), 'seq').astype(jnp.float32)]
    reduce_scatter x1, waiting for transfers between devices: 127 us -> 110 us  [shards(): lax.psum_scatter(jnp.concatenate([jnp.dot(gathered, gate_weight, preferre...]
    reduce_sum x0 -> x1, other arithmetic: none -> 9.96 us  [shards(): downs = jnp.sum(terms, axis=0)]
    all_gather x1, waiting for transfers between devices: 37.8 us -> 32 us  [shards(): gathered = lax.all_gather(tokens, 'tp', axis=0, tiled=True)]
  transfers between devices with their start and end apart: 5 -> 5, of which waited for: 4 -> 5; matrix products, arithmetic and copies ran while one was open for 13% -> 18% of each run, Pallas kernels for 0% -> 0%
where the time goes in v1:
time: 389 us; the launch traced here: 388 us
  waiting for transfers between devices  300 us (77%)
  other arithmetic  32.2 us (8%)
  matrix products  31.2 us (8%)
  between operations  13.2 us (3%)
  local copies, waits for them, and re-layouts  11.8 us (3%)
    reduce_scatter x1, waiting for transfers between devices, shards(): lax.psum_scatter(jnp.concatenate([jnp.dot(gathered, gate_weight, preferre...  110 us
    reduce_scatter x1, waiting for transfers between devices, shards(): lax.psum_scatter(table_up.astype(jnp.bfloat16), 'seq', scatter_dimension=...  69.5 us
    all_gather x1, waiting for transfers between devices, shards(): terms = lax.all_gather(block, 'tp')  53.9 us
    psum x1, waiting for transfers between devices, shards(): inner_total = lax.psum(flat.astype(jnp.bfloat16), 'seq').astype(jnp.float32)  33.5 us
    all_gather x1, waiting for transfers between devices, shards(): gathered = lax.all_gather(tokens, 'tp', axis=0, tiled=True)  32 us
    dot_general x1, matrix products, shards(): jnp.dot(gathered, up_weight, preferred_element_type=jnp.float32)  13 us
    dot_general x1, matrix products, shards(): jnp.dot(gathered, gate_weight, preferred_element_type=jnp.float32)  12.4 us
    reduce_sum x1, other arithmetic, shards(): downs = jnp.sum(terms, axis=0)  9.96 us
  transfers between devices with their start and end apart: 5, of which 5 were waited for; matrix products, arithmetic and copies ran while one was open for 18% of the time, Pallas kernels for 0%

profile of v1, /device:TPU:0, one launch (start us, length us, event | category | flops | bytes accessed | tf_op | source)
XLA Modules:
  0.0 388.5 jit_solution(17335427273976487903)
XLA Ops:
  6.5 0.7 all-gather.3.cloned.1.call-update
  7.3 0.8 reduce-window.8
  8.2 1.3 gather_fusion
  9.6 1.3 gather_fusion.1
  10.9 2.1 gather_fusion.2
  13.0 3.6 select_convert_fusion.1
  16.7 32.0 %all-gather.3.cloned.1.call-done = bf16[1024,2048]{1,0:T(8,128)(2,1)} async-done(((bf16[128,2048]{1,0:T(8,128)(2,1)}), bf16[1024,2048]{1,0:T(8,128)(2,1)}) %all-gather.3.cloned.1.call-update) | async-done | bytes 4194320 | tf_op jit(solution)/shard_map/all_gather | solution.py:41
  48.7 13.0 %convolution_convert_fusion = bf16[1024,1792]{1,0:T(8,128)(2,1)} fusion(bf16[1024,2048]{1,0:T(8,128)(2,1)} %all-gather.3.cloned.1.call-done, bf16[2048,1792]{1,0:T(8,128)(2,1)} %param.10), kind=kOutput, calls=%fused_computation.7 | convolution fusion | flops 7518027776 | bytes 15204352 | tf_op jit(solution)/shard_map/dot_general | solution.py:61
  61.7 12.4 %convolution_convert_fusion.1 = bf16[1024,1792]{1,0:T(8,128)(2,1)} fusion(bf16[1024,2048]{1,0:T(8,128)(2,1)S(1)} %copy-done.3, bf16[2048,1792]{1,0:T(8,128)(2,1)} %param.9), kind=kOutput, calls=%fused_computation.8 | convolution fusion | flops 7518027776 | bytes 15204352 | tf_op jit(solution)/shard_map/dot_general | solution.py:60
  74.1 6.6 %pad_maximum_fusion = bf16[1024,3584]{1,0:T(8,128)(2,1)} fusion(bf16[1024,1792]{1,0:T(8,128)(2,1)} %convolution_convert_fusion, bf16[1024,1792]{1,0:T(8,128)(2,1)} %convolution_convert_fusion.1), kind=kLoop, calls=%fused_computation.4 | loop fusion | flops 14680064 | bytes 14680064 | tf_op jit(solution)/shard_map/concatenate | solution.py:58
  80.9 5.7 %gather_fusion.3 = bf16[8,2,64,1792]{3,2,1,0:T(8,128)(2,1)} fusion(bf16[16,2,64,1792]{3,2,1,0:T(8,128)(2,1)} %param.12, s32[1024]{0:T(1024)S(1)} %pad_clamp_fusion), kind=kCustom, calls=%fused_computation.3 | custom fusion | bytes 7340064 | tf_op jit(solution)/shard_map/jit(_take)/gather | solution.py:36
  86.6 53.9 %all-gather.5.cloned.1.call-done = bf16[8,8,64,2048]{3,2,1,0:T(8,128)(2,1)} async-done(((bf16[1,8,64,2048]{3,2,1,0:T(8,128)(2,1)}), bf16[8,8,64,2048]{3,2,1,0:T(8,128)(2,1)}) %all-gather.5.cloned.1.call-update) | async-done | bytes 16777232 | tf_op jit(solution)/shard_map/all_gather | solution.py:33
  140.5 10.0 %reduce_sum.25 = bf16[8,64,2048]{2,1,0:T(8,128)(2,1)S(1)} reduce(bf16[8,8,64,2048]{3,2,1,0:T(8,128)(2,1)} %all-gather.5.cloned.1.call-done, bf16[]{:T(256)} %constant.121.clone.1), dimensions={0}, to_apply=%region_3.4 | reduce | flops 7340032 | bytes 18874370 | tf_op jit(solution)/shard_map/reduce_sum | solution.py:34
  150.4 3.8 fusion.6
  154.4 0.8 convert_element_type.61
  155.5 4.9 %select_convert_fusion = bf16[8,2,64,1792]{3,2,1,0:T(8,128)(2,1)} fusion(bf16[8,2,64,1792]{3,2,1,0:T(8,128)(2,1)} %gather_fusion.3, pred[8]{0:T(512)(128)(4,1)S(1)} %get-tuple-element.10, pred[8]{0:T(512)(128)(4,1)S(1)} %get-tuple-element.11), kind=kLoop, calls=%fused_computation.5 | loop fusion | flops 7340032 | bytes 7340048 | tf_op jit(solution)/shard_map/convert_element_type | solution.py:39
  160.4 110.1 %reduce-scatter.3.cloned.1.call-done = bf16[256,3584]{1,0:T(8,128)(2,1)} async-done(((bf16[1024,3584]{1,0:T(8,128)(2,1)}), bf16[256,3584]{1,0:T(8,128)(2,1)}) %reduce-scatter.3.cloned.1.call-update) | async-done | bytes 1835024 | tf_op jit(solution)/shard_map/reduce_scatter | solution.py:57
  270.6 3.7 convert_element_type.55
  274.3 33.5 %all-reduce.2.cloned.1.call-done = bf16[512,128]{1,0:T(8,128)(2,1)} async-done(((bf16[512,128]{1,0:T(8,128)(2,1)}), bf16[512,128]{1,0:T(8,128)(2,1)}) %all-reduce.2.cloned.1.call-update) | async-done | bytes 131088 | tf_op jit(solution)/shard_map/psum | solution.py:51
  307.7 0.8 convert_convert_fusion
  308.6 69.5 %reduce-scatter.5.cloned.1.call-done = bf16[2,2,64,1792]{3,2,1,0:T(8,128)(2,1)} async-done(((bf16[8,2,64,1792]{3,2,1,0:T(8,128)(2,1)}), bf16[2,2,64,1792]{3,2,1,0:T(8,128)(2,1)}) %reduce-scatter.5.cloned.1.call-update) | async-done | bytes 917520 | tf_op jit(solution)/shard_map/reduce_scatter | solution.py:38
  378.1 1.9 fusion.7
  380.0 0.4 copy-done.2
  380.4 1.5 fusion.3
  (29 shorter events, 0.9 us)
Async XLA Ops:
  6.5 4.4 %copy-start = (bf16[8,64,2048]{2,1,0:T(8,128)(2,1)S(1)}, bf16[8,64,2048]{2,1,0:T(8,128)(2,1)}, u32[]{:S(2)}) copy-start(bf16[8,64,2048]{2,1,0:T(8,128)(2,1)} %param.11) | copy-start | bytes 6291460
  6.5 42.2 %all-gather.3.cloned.1.call-start = ((), (), s32[]{:S(2)}) async-start(), calls=%async_computation.2 | async-start | bytes 4718592 | tf_op jit(solution)/shard_map/all_gather | solution.py:41
  7.3 133.2 %all-gather.5.cloned.1.call-start = ((), (), s32[]{:S(2)}) async-start(), calls=%async_computation.4 | async-start | bytes 18874368 | tf_op jit(solution)/shard_map/all_gather | solution.py:33
  16.7 253.9 %reduce-scatter.3.cloned.1.call-start = ((), (), s32[]{:S(2)}) async-start(), calls=%async_computation.3 | async-start | bytes 9175040 | tf_op jit(solution)/shard_map/reduce_scatter | solution.py:57
  48.7 13.0 %copy-start.3 = (bf16[1024,2048]{1,0:T(8,128)(2,1)S(1)}, bf16[1024,2048]{1,0:T(8,128)(2,1)}, u32[]{:S(2)}) copy-start(bf16[1024,2048]{1,0:T(8,128)(2,1)} %all-gather.3.cloned.1.call-done) | copy-start | bytes 12582916
  80.8 227.0 %all-reduce.2.cloned.1.call-start = ((), (), s32[]{:S(2)}) async-start(), calls=%async_computation.5 | async-start | bytes 262144 | tf_op jit(solution)/shard_map/psum | solution.py:51
  155.2 222.8 %reduce-scatter.5.cloned.1.call-start = ((), (), s32[]{:S(2)}) async-start(), calls=%async_computation.6 | async-start | bytes 4587520 | tf_op jit(solution)/shard_map/reduce_scatter | solution.py:38
  378.1 2.3 copy-start.2
  380.0 1.9 copy-start.1
Sparse Core Ops, SparseCore 0:
  9.2 39.4 all-gather.2
  50.6 89.8 all-gather.4
  142.8 127.7 reduce-scatter.2
  272.7 34.9 all-reduce.1
  310.0 68.0 reduce-scatter.4
